TPU v7x, 128 devices: a whole 4x4x4 slice. The times are simulated.
128 devices in a mesh: layer: 16 (over y_hi, z, core), feat: 2 (over y_lo), tok: 4 (over x).
Axes of the slice: x: 4, y: 4 (y_hi: 2, y_lo: 2; y = y_hi * 2 + y_lo), z: 4, core: 2. Of those that a mesh axis runs over, the one named last changes fastest.
Arguments:
- sublevel_entries: bfloat16 [16, 1024, 1152], P('layer', 'tok'), may hold values from -6 to 6
- readin_matrix: bfloat16 [16, 1152, 8192], P('layer', None, ('feat', 'tok')), may hold values from -0.1875 to 0.1875
- readin_offset: float32 [16, 8192], P('layer', ('feat', 'tok')), may hold values from -3 to 3
- cutoff_exceeded: int32 [16, 1024, 8192], P('layer', None, ('feat', 'tok')), may hold values 0 or 1
- writeout_matrix: bfloat16 [16, 2, 8192, 1152], P('layer', None, ('feat', 'tok')), may hold values from -0.0625 to 0.0625
- hidden_block_result: bfloat16 [2, 1024, 1152], P(None, 'tok'), may hold values from -6 to 6
- writing_depth_number: int32 [2], replicated, may hold values from 0 to 15, as said below
Outputs:
- enc_grad: bfloat16 [16, 1152, 8192], P('layer', None, ('feat', 'tok'))
- dec_grad: bfloat16 [16, 2, 8192, 1152], P('layer', None, ('feat', 'tok'))
- bias_grad: float32 [16, 8192], P('layer', ('feat', 'tok'))
Inputs may be any that keep to these rules, and one draw needn't show every extreme that they name: `writing_depth_number`: one of the two entries is 15 and the other is smaller; either may come first.
All inputs are finite; a program needn't handle non-finite values. No bound on the sum of `cutoff_exceeded` on one device may be relied on, other than what follows from the above.
Results may differ from a plain program's by a relative error of at most 0.007.
Values may be sent and summed in bfloat16 or wider, within the bound.
A program may use at most 128 MiB of HBM per device.

v0:
```python
import math

import jax
import jax.numpy as jnp
from jax import lax
from jax.sharding import PartitionSpec as P


def shards(
    sublevel_entries,
    readin_matrix,
    readin_offset,
    cutoff_exceeded,
    writeout_matrix,
    hidden_block_result,
    writing_depth_number,
):
    layer_index = lax.axis_index("layer")
    owner_flag = jnp.logical_and(layer_index == 0, lax.axis_index("feat") == 0).astype(jnp.float32)
    gathered = lax.all_gather(sublevel_entries, "tok", axis=1, tiled=True)[0]
    total_rows = gathered.shape[0]
    inverse = 1.0 / math.sqrt(total_rows)
    gate_choice_vector = cutoff_exceeded[0].astype(jnp.float32)
    encoded_prejump_signal = (
        jnp.dot(gathered, readin_matrix[0], preferred_element_type=jnp.float32)
        + readin_offset[0][None, :]
    )
    sparse_code_entries = (encoded_prejump_signal * gate_choice_vector).astype(jnp.bfloat16)
    live_mask = (layer_index <= writing_depth_number).astype(jnp.float32)
    target_count = writeout_matrix.shape[1]
    partials = jnp.stack(
        [
            jnp.dot(
                sparse_code_entries,
                writeout_matrix[0, desired_reconstruction],
                preferred_element_type=jnp.float32,
            )
            for desired_reconstruction in range(target_count)
        ]
    )
    goal_rows = hidden_block_result.shape[1]
    row_start = lax.axis_index("tok") * goal_rows
    current = lax.dynamic_slice_in_dim(partials, row_start, goal_rows, 1)
    partials = lax.dynamic_update_slice_in_dim(
        partials, current - owner_flag * hidden_block_result.astype(jnp.float32), row_start, 1
    )
    summed = lax.psum(partials * live_mask[:, None, None], ("layer", "feat", "tok"))
    scaled = (summed * inverse).astype(jnp.bfloat16)
    dec_rows = []
    code_sensitivity = jnp.zeros(encoded_prejump_signal.shape, jnp.float32)
    for desired_reconstruction in range(target_count):
        dec_rows.append(
            (
                jnp.einsum(
                    "tf,td->fd",
                    sparse_code_entries,
                    scaled[desired_reconstruction],
                    preferred_element_type=jnp.float32,
                )
                * live_mask[desired_reconstruction]
            ).astype(jnp.bfloat16)
        )
        code_sensitivity = code_sensitivity + live_mask[desired_reconstruction] * jnp.einsum(
            "td,fd->tf",
            scaled[desired_reconstruction],
            writeout_matrix[0, desired_reconstruction],
            preferred_element_type=jnp.float32,
        )
    prejump_sensitivity = code_sensitivity * gate_choice_vector
    bias_grad = jnp.sum(prejump_sensitivity, axis=0)
    enc_grad = jnp.einsum(
        "td,tf->df",
        gathered,
        prejump_sensitivity.astype(jnp.bfloat16),
        preferred_element_type=jnp.float32,
    ).astype(jnp.bfloat16)
    return (enc_grad[None], jnp.stack(dec_rows)[None], bias_grad[None])


def solution(mesh):
    return jax.shard_map(
        shards,
        mesh=mesh,
        in_specs=(
            P("layer", "tok", None),
            P("layer", None, ("feat", "tok")),
            P("layer", ("feat", "tok")),
            P("layer", None, ("feat", "tok")),
            P("layer", None, ("feat", "tok"), None),
            P(None, "tok", None),
            P(),
        ),
        out_specs=(
            P("layer", None, ("feat", "tok")),
            P("layer", None, ("feat", "tok"), None),
            P("layer", ("feat", "tok")),
        ),
        check_vma=False,
    )
```

profile of v0, /device:TPU:1, one launch (start us, length us, event | category | flops | bytes accessed | tf_op | source)
XLA Modules:
  0.0 273.5 jit_solution(17412441539697381192)
XLA Ops:
  7.2 0.0 copy-start
  7.2 0.0 all-gather.2.cloned.1.call-start
  7.2 0.7 all-gather.2.cloned.1.call-update
  7.9 0.0 all-reduce.2.cloned.1.call-start
  8.0 0.7 compare_convert_fusion
  8.6 37.0 %all-gather.2.cloned.1.call-done = bf16[1,1024,1152]{2,1,0:T(8,128)(2,1)} async-done(((bf16[1,256,1152]{2,1,0:T(8,128)(2,1)}), bf16[1,1024,1152]{2,1,0:T(8,128)(2,1)}) %all-gather.2.cloned.1.call-update) | async-done | bytes 2359312 | tf_op jit(solution)/shard_map/all_gather | solution.py:20
  45.6 0.0 copy-done
  45.6 0.0 copy-start.2
  45.6 5.6 %fusion = bf16[1024,1024]{1,0:T(8,128)(2,1)S(1)} fusion(s32[1,1024,1024]{2,1,0:T(8,128)} %param.10, f32[1024]{0:T(1024)} %bitcast.68, bf16[1,1152,1024]{2,1,0:T(8,128)(2,1)S(1)} %copy-done, bf16[1,1024,1152]{2,1,0:T(8,128)(2,1)} %all-gather.2.cloned.1.call-done), kind=kOutput, calls=%fused_computation.12 | convolution fusion | flops 2420113408 | bytes 11014144 | tf_op jit(solution)/shard_map/dot_general | solution.py:25
  51.2 0.0 copy-done.2
  51.2 0.0 copy-start.5
  51.2 2.9 %convolution_bitcast_fusion = f32[1,1024,1152]{2,1,0:T(8,128)S(1)} fusion(bf16[1024,1024]{1,0:T(8,128)(2,1)S(1)} %fusion, bf16[1,2,1024,1152]{3,2,1,0:T(8,128)(2,1)S(1)} %copy-done.2), kind=kOutput, calls=%fused_computation.8 | convolution fusion | flops 2415919104 | bytes 9175040 | tf_op jit(solution)/shard_map/dot_general | solution.py:33
  54.1 0.0 copy-done.5
  54.1 2.9 %convolution_bitcast_fusion.1 = f32[1,1024,1152]{2,1,0:T(8,128)S(1)} fusion(bf16[1024,1024]{1,0:T(8,128)(2,1)S(1)} %fusion, bf16[1,2,1024,1152]{3,2,1,0:T(8,128)(2,1)S(1)} %copy-done.2), kind=kOutput, calls=%fused_computation.9 | convolution fusion | flops 2415919104 | bytes 9175040 | tf_op jit(solution)/shard_map/dot_general | solution.py:33
  57.0 0.6 pad_maximum_fusion
  57.6 1.8 fusion.8
  59.4 4.3 %broadcast_multiply_fusion = f32[2,1024,1152]{2,1,0:T(8,128)} fusion(f32[2,1024,1152]{2,1,0:T(8,128)S(1)} %fusion.8, f32[2]{0:T(128)S(1)} %compare_convert_fusion), kind=kLoop, calls=%fused_computation.7 | loop fusion | flops 2359296 | bytes 18874376 | tf_op jit(solution)/shard_map/mul | solution.py:47
  63.7 0.0 all-reduce.2.cloned.1.call-update
  63.7 0.6 fusion.30
  64.3 163.7 %all-reduce.2.cloned.1.call-done = f32[2,1024,1152]{2,1,0:T(8,128)} async-done(((f32[2,1024,1152]{2,1,0:T(8,128)}), f32[2,1024,1152]{2,1,0:T(8,128)}) %all-reduce.2.cloned.1.call-update) | async-done | bytes 9437200 | tf_op jit(solution)/shard_map/psum | solution.py:47
  227.9 4.4 %multiply_convert_fusion = bf16[2,1024,1152]{2,1,0:T(8,128)(2,1)S(1)} fusion(f32[2,1024,1152]{2,1,0:T(8,128)} %all-reduce.2.cloned.1.call-done), kind=kLoop, calls=%fused_computation.3 | loop fusion | flops 4718592 | bytes 14155776 | tf_op jit(solution)/shard_map/convert_element_type | solution.py:48
  232.4 0.0 copy-start.6
  232.4 4.7 %fusion.9 = f32[1024,1024]{1,0:T(8,128)S(1)} fusion(bf16[2,1024,1152]{2,1,0:T(8,128)(2,1)S(1)} %multiply_convert_fusion, bf16[1,2,1024,1152]{3,2,1,0:T(8,128)(2,1)} %param.11), kind=kOutput, calls=%fused_computation.24 | convolution fusion | flops 2415919104 | bytes 8912896 | tf_op jit(solution)/shard_map/td,fd->tf/dot_general | solution.py:63
  237.1 0.0 copy-done.6
  237.1 0.0 slice-start
  237.1 5.0 %fusion.4 = bf16[1,1024,1152]{2,1,0:T(8,128)(2,1)} fusion(bf16[1024,1024]{1,0:T(8,128)(2,1)S(1)} %copy-done.6, f32[]{:T(128)} %bitcast.10, bf16[2,1024,1152]{2,1,0:T(8,128)(2,1)S(1)} %multiply_convert_fusion), kind=kOutput, calls=%fused_computation.17 | convolution fusion | flops 2418278400 | bytes 6815748 | tf_op jit(solution)/shard_map/tf,td->fd/dot_general | solution.py:54
  242.1 0.0 slice-start.1
  242.1 0.0 copy-start.3
  242.1 5.2 %fusion.5 = bf16[1,1024,1152]{2,1,0:T(8,128)(2,1)} fusion(bf16[1024,1024]{1,0:T(8,128)(2,1)S(1)} %copy-done.6, f32[]{:T(128)} %bitcast, bf16[2,1024,1152]{2,1,0:T(8,128)(2,1)S(1)} %multiply_convert_fusion), kind=kOutput, calls=%fused_computation.18 | convolution fusion | flops 2418278400 | bytes 6815748 | tf_op jit(solution)/shard_map/tf,td->fd/dot_general | solution.py:54
  247.4 0.0 slice-done
  247.4 0.0 slice-done.1
  247.4 0.0 copy-done.3
  247.4 0.0 copy-start.4
  247.4 5.6 %fusion.31 = (f32[1024]{0:T(1024)}, bf16[1024,1024]{1,0:T(8,128)(2,1)S(1)}) fusion(s32[1,1024,1024]{2,1,0:T(8,128)S(1)} %copy-done.3, f32[1024,1024]{1,0:T(8,128)S(1)} %fusion.9, f32[]{:T(128)} %bitcast.10, bf16[1,2,1024,1152]{3,2,1,0:T(8,128)(2,1)S(1)} %bitcast.67, bf16[2,1024,1152]{2,1,0:T(8,128)(2,1)S(1)} %multiply_convert_fusion, f32[]{:T(128)} %bitcast), kind=kOutput, calls=%fused_computation.41 | convolution fusion | flops 2423258112 | bytes 15208456 | tf_op jit(solution)/shard_map/td,fd->tf/dot_general | solution.py:63
  253.0 0.0 copy-done.4
  253.0 4.2 %fusion.3 = bf16[1,1152,1024]{1,2,0:T(8,128)(2,1)} fusion(bf16[1,1024,1152]{2,1,0:T(8,128)(2,1)S(1)} %copy-done.4, bf16[1024,1024]{1,0:T(8,128)(2,1)S(1)} %get-tuple-element.9), kind=kOutput, calls=%fused_computation.16 | convolution fusion | flops 2417098752 | bytes 6815744 | tf_op jit(solution)/shard_map/td,tf->df/dot_general | solution.py:71
  257.2 0.0 copy-start.1
  257.2 4.4 %copy.10 = bf16[1,1152,1024]{2,1,0:T(8,128)(2,1)} copy(bf16[1,1152,1024]{1,2,0:T(8,128)(2,1)} %fusion.3) | data formatting | bytes 4718592
  261.6 5.0 %maximum_bitcast_fusion = bf16[1,2,1024,1152]{3,2,1,0:T(8,128)(2,1)} fusion(bf16[1,1024,1152]{2,1,0:T(8,128)(2,1)} %fusion.4, bf16[1,1024,1152]{2,1,0:T(8,128)(2,1)} %fusion.5), kind=kLoop, calls=%fused_computation.6 | loop fusion | flops 2359296 | bytes 9437184 | tf_op jit(solution)/shard_map/broadcast_in_dim | solution.py:77
  266.6 0.0 copy-done.1
  (1 shorter events, 0.0 us)
Async XLA Ops:
  7.2 38.5 %copy-start = (bf16[1,1152,1024]{2,1,0:T(8,128)(2,1)S(1)}, bf16[1,1152,1024]{2,1,0:T(8,128)(2,1)}, u32[]{:S(2)}) copy-start(bf16[1,1152,1024]{2,1,0:T(8,128)(2,1)} %param.8) | copy-start | bytes 7077892
  7.2 38.4 %all-gather.2.cloned.1.call-start = ((), (), s32[]{:S(2)}) async-start(), calls=%async_computation | async-start | bytes 2949120 | tf_op jit(solution)/shard_map/all_gather | solution.py:20
  7.9 220.0 %all-reduce.2.cloned.1.call-start = ((), (), s32[]{:S(2)}) async-start(), calls=%async_computation.1 | async-start | bytes 18874368 | tf_op jit(solution)/shard_map/psum | solution.py:47
  45.6 5.6 %copy-start.2 = (bf16[1,2,1024,1152]{3,2,1,0:T(8,128)(2,1)S(1)}, bf16[1,2,1024,1152]{3,2,1,0:T(8,128)(2,1)}, u32[]{:S(2)}) copy-start(bf16[1,2,1024,1152]{3,2,1,0:T(8,128)(2,1)} %param.11) | copy-start | bytes 14155780
  51.2 2.9 %copy-start.5 = (bf16[1024,1024]{1,0:T(8,128)(2,1)}, bf16[1024,1024]{1,0:T(8,128)(2,1)S(1)}, u32[]{:S(2)}) copy-start(bf16[1024,1024]{1,0:T(8,128)(2,1)S(1)} %fusion) | copy-start | bytes 6291460
  232.4 4.7 %copy-start.6 = (bf16[1024,1024]{1,0:T(8,128)(2,1)S(1)}, bf16[1024,1024]{1,0:T(8,128)(2,1)}, u32[]{:S(2)}) copy-start(bf16[1024,1024]{1,0:T(8,128)(2,1)} %copy-done.5) | copy-start | bytes 6291460
  237.1 10.3 %slice-start = ((s8[4718592]{0:T(1024)(128)(4,1)}), s8[4194304]{0:T(1024)(128)(4,1)S(1)}, s32[]{:S(2)}) async-start(s8[4718592]{0:T(1024)(128)(4,1)} %bitcast.66), calls=%async_computation.2 | async-start | bytes 8388608
  242.1 5.3 %slice-start.1 = ((s8[4718592]{0:T(1024)(128)(4,1)}), s8[524288]{0:T(1024)(128)(4,1)S(1)}, s32[]{:S(2)}) async-start(s8[4718592]{0:T(1024)(128)(4,1)} %bitcast.66), calls=%async_computation.3 | async-start | bytes 1048576
  242.1 5.3 %copy-start.3 = (s32[1,1024,1024]{2,1,0:T(8,128)S(1)}, s32[1,1024,1024]{2,1,0:T(8,128)}, u32[]{:S(2)}) copy-start(s32[1,1024,1024]{2,1,0:T(8,128)} %param.10) | copy-start | bytes 12582916
  247.4 5.6 %copy-start.4 = (bf16[1,1024,1152]{2,1,0:T(8,128)(2,1)S(1)}, bf16[1,1024,1152]{2,1,0:T(8,128)(2,1)}, u32[]{:S(2)}) copy-start(bf16[1,1024,1152]{2,1,0:T(8,128)(2,1)} %all-gather.2.cloned.1.call-done) | copy-start | bytes 7077892
  257.2 9.5 %copy-start.1 = (bf16[1,1152,1024]{2,1,0:T(8,128)(2,1)S(1)}, bf16[1,1152,1024]{2,1,0:T(8,128)(2,1)}, u32[]{:S(2)}) copy-start(bf16[1,1152,1024]{2,1,0:T(8,128)(2,1)} %param.8) | copy-start | bytes 7077892
Sparse Core Ops, SparseCore 0:
  9.6 35.9 all-gather.1
  63.8 164.0 all-reduce.1
where the time goes:
time: 274 us; the launch traced here: 273 us
  waiting for transfers between devices  201 us (73%)
  matrix products  36 us (13%)
  other arithmetic  16.8 us (6%)
  between operations  14.2 us (5%)
  local copies, waits for them, and re-layouts  5.04 us (2%)
    psum x1, waiting for transfers between devices, shards(): lax.psum(partials * live_mask[:, None, None], ('layer', 'feat', 'tok'))  164 us
    all_gather x1, waiting for transfers between devices, shards(): gathered = lax.all_gather(sublevel_entries, 'tok', axis=1, tiled=True)[0]  37 us
    dot_general x2, matrix products, shards(): jnp.einsum('td,fd->tf', scaled[desired_reconstruction], writeout_matrix[0...  10.3 us
    dot_general x2, matrix products, shards(): jnp.einsum('tf,td->fd', sparse_code_entries, scaled[desired_reconstructio...  10.2 us
    dot_general x2, matrix products, shards(): jnp.dot(sparse_code_entries, writeout_matrix[0, desired_reconstruction],...  5.74 us
    dot_general x1, matrix products, shards(): jnp.dot(gathered, readin_matrix[0], preferred_element_type=jnp.float32)  5.56 us
  transfers between devices with their start and end apart: 2, of which 2 were waited for; matrix products, arithmetic and copies ran while one was open for 0% of the time, Pallas kernels for 0%

commit v1 on v0

v1 whole, which is shorter than its diff:
```python
import functools
import math

import jax
import jax.numpy as jnp
from jax import lax
from jax.experimental import pallas as pl
from jax.experimental.pallas import tpu as pltpu
from jax.sharding import PartitionSpec as P

MESH = pl.DeviceIdType.MESH
F32, BF16 = jnp.float32, jnp.bfloat16
ROUNDS = 4
NT = (((1,), (1,)), ((), ()))
TN = (((0,), (0,)), ((), ()))
GAP = {"F": 0.0, "E": 4.8, "1": 9.3, "2": 15.1, "3": 17.8, "4": 20.6, "5": 23.1, "6": 28.6, "7": 31.1}
PERIOD = 4.9


def sent(R):
    slots = {}
    for name, count in (("g", 4), ("p", 1), ("a1", 3), ("b1", 3), ("a2", 3), ("b2", 3), ("x", 3),
                        ("ga1", 3), ("gb1", 3), ("ga2", 3), ("gb2", 3), ("fa", 1), ("fb", 1)):
        for i in range(count):
            slots[name, i] = len(slots)
    return slots


def comm_kernel(cfg, live_ref, x_hbm, wr_hbm, off_ref, gate_hbm, wo_hbm, hid_hbm,
                bias_ref, g_out, acts_out, low_out, sa_out, sb_out,
                g, wr, gate, wo, hid, acts, low, pk, cs, cr, s1a, s1b, r1a, r1b, k2a, k2b, s2a, s2b, r2a, r2b,
                k3, s3, r3, sa, sb, send_sem, recv_sem, in_sem, own_sem, out_sem):
    R, TB, D, DA, Fw, inverse = cfg
    DB = D - DA
    M, PR, HB = 4 * TB, TB // 4, TB // 2
    slots = sent(R)
    layer, feat, x = lax.axis_index("layer"), lax.axis_index("feat"), lax.axis_index("tok")
    c = lax.rem(layer, 2)
    z = lax.rem(lax.div(layer, 2), 4)
    y = lax.div(layer, 8) * 2 + feat
    other = 1 - c

    def xpeer(o):
        return (layer, feat, lax.rem(x + o, 4))

    def zpeer(o):
        return (lax.div(layer, 8) * 8 + lax.rem(z + o, 4) * 2 + c, feat, x)

    def ypeer(o):
        yy = lax.rem(y + o, 4)
        return (lax.div(yy, 2) * 8 + z * 2 + c, lax.rem(yy, 2), x)

    partner = (lax.div(layer, 2) * 2 + other, feat, x)

    def at(index, size):
        return pl.ds(pl.multiple_of(index * size, size), size)

    def remote(j, name, i, src, dst, device):
        k = slots[name, i]
        return pltpu.make_async_remote_copy(
            src_ref=src, dst_ref=dst, send_sem=send_sem.at[j, k], recv_sem=recv_sem.at[j, k],
            device_id=device, device_id_type=MESH)

    started = []

    def send(j, name, i, src, dst, device):
        copy = remote(j, name, i, src, dst, device)
        copy.start()
        started.append(copy)

    def arrive(j, name, i, dst):
        remote(j, name, i, dst, dst, partner).wait_recv()

    loads = [pltpu.make_async_copy(a, b, in_sem.at[i]) for i, (a, b) in enumerate(
        ((wr_hbm, wr), (gate_hbm, gate), (wo_hbm, wo), (hid_hbm, hid)))]
    own = [pltpu.make_async_copy(x_hbm.at[pl.ds(j * TB, TB)], g.at[j, at(x, TB)], own_sem.at[j]) for j in range(R)]
    for j in range(R):
        own[j].start()
    for copy in loads:
        copy.start()
    bias_ref[...] = jnp.zeros_like(bias_ref)

    barrier = pltpu.get_barrier_semaphore()
    peers = [p(o) for p in (xpeer, ypeer, zpeer) for o in (1, 3, 2)] + [partner]
    for p in peers:
        pl.semaphore_signal(barrier, inc=1, device_id=p, device_id_type=MESH)
    pl.semaphore_wait(barrier, len(peers))

    def gather_own(j):
        src = x_hbm.at[pl.ds(j * TB, TB)]
        send(j, "g", 0, src, g.at[j, at(x, TB)], xpeer(1))
        send(j, "g", 1, src, g.at[j, at(x, TB)], xpeer(3))

    outs = []

    def put(src, dst):
        copy = pltpu.make_async_copy(src, dst, out_sem.at[len(outs)])
        copy.start()
        outs.append(copy)

    def stage_f(j):
        left, right = lax.rem(x + 3, 4), lax.rem(x + 1, 4)
        arrive(j, "g", 0, g.at[j, at(left, TB)])
        rows = pl.ds(pl.multiple_of(left * TB, TB), HB)
        send(j, "g", 2, g.at[j, rows], g.at[j, rows], xpeer(1))
        arrive(j, "g", 1, g.at[j, at(right, TB)])
        rows = pl.ds(pl.multiple_of(right * TB + HB, HB), HB)
        send(j, "g", 3, g.at[j, rows], g.at[j, rows], xpeer(3))
        if j + 2 < R:
            gather_own(j + 2)

    def stage_e(j):
        far = lax.rem(x + 2, 4)
        arrive(j, "g", 2, g.at[j, pl.ds(pl.multiple_of(far * TB, TB), HB)])
        arrive(j, "g", 3, g.at[j, pl.ds(pl.multiple_of(far * TB + HB, HB), HB)])
        own[j].wait()
        put(g.at[j], g_out.at[j])
        if j == 0:
            loads[0].wait()
            loads[1].wait()

        @pl.loop(0, Fw // 256)
        def _(n):
            cols = pl.ds(pl.multiple_of(n * 256, 256), 256)
            pre = jnp.dot(g[j], wr[:, cols], preferred_element_type=F32) + off_ref[:, cols]
            for t in range(4):
                rows = slice(t * TB, (t + 1) * TB)
                acts[j, rows, cols] = (pre[rows] * gate[t, j * TB:(j + 1) * TB, cols].astype(F32)).astype(BF16)

        if j == 0:
            loads[2].wait()

        @pl.loop(0, D // 384)
        def _(n):
            cols = pl.ds(pl.multiple_of(n * 384, 128), 384)
            part = jnp.dot(acts[j], wo[other, :, cols], preferred_element_type=F32)
            cs[j, :, cols] = (part * live_ref[other]).astype(BF16)

        send(j, "p", 0, cs.at[j], cr.at[j], partner)
        put(acts.at[j], acts_out.at[j])

        @pl.loop(0, D // 384)
        def _(n):
            cols = pl.ds(pl.multiple_of(n * 384, 128), 384)
            part = jnp.dot(acts[j], wo[c, :, cols], preferred_element_type=F32)
            pk[j, :, cols] = part * live_ref[c]

    def stage_1(j):
        arrive(j, "p", 0, cr.at[j])
        s1a[j] = (pk[j, :, :DA] + cr[j, :, :DA].astype(F32)).astype(BF16)
        for o in (2, 1, 3):
            send(j, "a1", o - 1, s1a.at[j, at(lax.rem(z + o, 4), TB)], r1a.at[j, o - 1], zpeer(o))
        s1b[j] = (pk[j, :, DA:] + cr[j, :, DA:].astype(F32)).astype(BF16)
        for o in (2, 1, 3):
            send(j, "b1", o - 1, s1b.at[j, at(lax.rem(y + o, 4), TB)], r1b.at[j, o - 1], ypeer(o))

    def stage_2(j):
        for name, r1, q, k2, s2, r2, lanes, p, me, out in (
                ("a1", r1a, z, k2a, s2a, r2a, slice(0, DA), ypeer, y, "a2"),
                ("b1", r1b, y, k2b, s2b, r2b, slice(DA, D), zpeer, z, "b2")):
            total = pk[j, at(q, TB), lanes] + cr[j, at(q, TB), lanes].astype(F32)
            for i in (0, 2, 1):
                arrive(j, name, i, r1.at[j, i])
                total = total + r1[j, i].astype(F32)
            k2[j] = total
            s2[j] = total.astype(BF16)
            for o in (2, 1, 3):
                send(j, out, o - 1, s2.at[j, at(lax.rem(me + o, 4), PR)], r2.at[j, o - 1], p(o))

    def stage_3(j):
        if j == 0:
            loads[3].wait()
        for name, r2, me, k2, lanes, q in (("a2", r2a, y, k2a, slice(0, DA), z), ("b2", r2b, z, k2b, slice(DA, D), y)):
            total = k2[j, at(me, PR)]
            for i in (0, 2, 1):
                arrive(j, name, i, r2.at[j, i])
                total = total + r2[j, i].astype(F32)
            owner = (q == x).astype(F32)
            total = total - owner * hid[c, pl.ds(pl.multiple_of(j * TB + me * PR, PR), PR), lanes].astype(F32)
            k3[j, :, lanes] = total
            s3[j, :, lanes] = total.astype(BF16)
        for o in (2, 1, 3):
            send(j, "x", o - 1, s3.at[j], r3.at[j, o - 1], xpeer(o))

    def stage_4(j):
        total = k3[j]
        for i in (0, 2, 1):
            arrive(j, "x", i, r3.at[j, i])
            total = total + r3[j, i].astype(F32)
        scaled = (total * inverse).astype(BF16)
        arows = pl.ds(pl.multiple_of(z * TB + y * PR, PR), PR)
        brows = pl.ds(pl.multiple_of(y * TB + z * PR, PR), PR)
        sa[c, j, arows] = scaled[:, :DA]
        sb[c, j, brows] = scaled[:, DA:]
        for o in (2, 1, 3):
            send(j, "ga1", o - 1, sa.at[c, j, arows], sa.at[c, j, arows], ypeer(o))
            send(j, "gb1", o - 1, sb.at[c, j, brows], sb.at[c, j, brows], zpeer(o))

    def stage_5(j):
        for i, o in ((0, 3), (2, 1), (1, 2)):
            yy, zz = lax.rem(y + o, 4), lax.rem(z + o, 4)
            arrive(j, "ga1", i, sa.at[c, j, pl.ds(pl.multiple_of(z * TB + yy * PR, PR), PR)])
            arrive(j, "gb1", i, sb.at[c, j, pl.ds(pl.multiple_of(y * TB + zz * PR, PR), PR)])
        for o in (2, 1, 3):
            send(j, "ga2", o - 1, sa.at[c, j, at(z, TB)], sa.at[c, j, at(z, TB)], zpeer(o))
            send(j, "gb2", o - 1, sb.at[c, j, at(y, TB)], sb.at[c, j, at(y, TB)], ypeer(o))

    def stage_6(j):
        for i, o in ((0, 3), (2, 1), (1, 2)):
            yy, zz = lax.rem(y + o, 4), lax.rem(z + o, 4)
            arrive(j, "ga2", i, sa.at[c, j, at(zz, TB)])
            arrive(j, "gb2", i, sb.at[c, j, at(yy, TB)])
        send(j, "fa", 0, sa.at[c, j], sa.at[c, j], partner)
        send(j, "fb", 0, sb.at[c, j], sb.at[c, j], partner)
        put(sa.at[c, j], sa_out.at[c, j])
        put(sb.at[c, j], sb_out.at[c, j])

    def stage_7(j):
        arrive(j, "fa", 0, sa.at[other, j])
        arrive(j, "fb", 0, sb.at[other, j])
        put(sa.at[other, j], sa_out.at[other, j])
        put(sb.at[other, j], sb_out.at[other, j])

        @pl.loop(0, Fw // 256)
        def _(n):
            cols = pl.ds(pl.multiple_of(n * 256, 256), 256)
            total = jnp.zeros((M, 256), F32)
            for t in range(2):
                part = lax.dot_general(sa[t, j], wo[t, cols, :DA], NT, preferred_element_type=F32)
                part = part + lax.dot_general(sb[t, j], wo[t, cols, DA:], NT, preferred_element_type=F32)
                total = total + live_ref[t] * part
            for t in range(4):
                rows = slice(t * TB, (t + 1) * TB)
                pre = total[rows] * gate[t, j * TB:(j + 1) * TB, cols].astype(F32)
                bias_ref[:, cols] += jnp.sum(pre, axis=0, keepdims=True)
                low[j, rows, cols] = pre.astype(BF16)

        put(low.at[j], low_out.at[j])

    gather_own(0)
    if R > 1:
        gather_own(1)
    stages = {"F": stage_f, "E": stage_e, "1": stage_1, "2": stage_2, "3": stage_3, "4": stage_4, "5": stage_5,
              "6": stage_6, "7": stage_7}
    order = sorted(((PERIOD * j + gap, s, j) for s, gap in GAP.items() for j in range(R)))
    for _, s, j in order:
        stages[s](j)
    for copy in started:
        copy.wait_send()
    for copy in outs:
        copy.wait()


def dec_kernel(live_ref, acts_ref, sa_ref, sb_ref, out_ref):
    DA = sa_ref.shape[-1]
    for t in range(2):
        for ref, lanes in ((sa_ref, slice(0, DA)), (sb_ref, slice(DA, out_ref.shape[-1]))):
            got = lax.dot_general(acts_ref[...], ref[t], TN, preferred_element_type=F32)
            out_ref[t, :, lanes] = (got * live_ref[t]).astype(BF16)


def enc_kernel(x_ref, low_ref, out_ref):
    out_ref[...] = lax.dot_general(x_ref[...], low_ref[...], TN, preferred_element_type=F32).astype(BF16)


def step(entries, readin, offset, cutoff, writeout, hidden, depths):
    R = ROUNDS
    tokens, D = entries.shape[1] * 4, entries.shape[2]
    Fw = readin.shape[2]
    TB = tokens // 4 // R
    M, PR, DA = 4 * TB, TB // 4, 640
    DB = D - DA
    live = (lax.axis_index("layer") <= depths).astype(F32)
    cfg = (R, TB, D, DA, Fw, 1.0 / math.sqrt(tokens))
    n_slots = len(sent(R))
    hbm = pl.BlockSpec(memory_space=pl.ANY)
    vmem = pl.BlockSpec(memory_space=pltpu.VMEM)
    smem = pl.BlockSpec(memory_space=pltpu.SMEM)
    V = pltpu.VMEM
    bias, g, acts, low, sa, sb = pl.pallas_call(
        functools.partial(comm_kernel, cfg),
        out_shape=(
            jax.ShapeDtypeStruct((1, Fw), F32),
            jax.ShapeDtypeStruct((R, M, D), BF16),
            jax.ShapeDtypeStruct((R, M, Fw), BF16),
            jax.ShapeDtypeStruct((R, M, Fw), BF16),
            jax.ShapeDtypeStruct((2, R, M, DA), BF16),
            jax.ShapeDtypeStruct((2, R, M, DB), BF16),
        ),
        in_specs=[smem, hbm, hbm, vmem, hbm, hbm, hbm],
        out_specs=(vmem, hbm, hbm, hbm, hbm, hbm),
        scratch_shapes=[
            V((R, M, D), BF16), V((D, Fw), BF16), V((4, tokens // 4, Fw), jnp.int32), V((2, Fw, D), BF16),
            V((2, tokens // 4, D), BF16), V((R, M, Fw), BF16), V((R, M, Fw), BF16),
            V((R, M, D), F32), V((R, M, D), BF16), V((R, M, D), BF16),
            V((R, M, DA), BF16), V((R, M, DB), BF16), V((R, 3, TB, DA), BF16), V((R, 3, TB, DB), BF16),
            V((R, TB, DA), F32), V((R, TB, DB), F32), V((R, TB, DA), BF16), V((R, TB, DB), BF16),
            V((R, 3, PR, DA), BF16), V((R, 3, PR, DB), BF16),
            V((R, PR, D), F32), V((R, PR, D), BF16), V((R, 3, PR, D), BF16),
            V((2, R, M, DA), BF16), V((2, R, M, DB), BF16),
            pltpu.SemaphoreType.DMA((R, n_slots)), pltpu.SemaphoreType.DMA((R, n_slots)),
            pltpu.SemaphoreType.DMA((4,)), pltpu.SemaphoreType.DMA((R,)), pltpu.SemaphoreType.DMA((7 * R,)),
        ],
        compiler_params=pltpu.CompilerParams(collective_id=0, has_side_effects=True, vmem_limit_bytes=60 * 2**20),
    )(live, entries[0], readin[0], offset, cutoff.reshape(4, tokens // 4, Fw), writeout[0], hidden)

    acts2, low2, g2 = acts.reshape(tokens, Fw), low.reshape(tokens, Fw), g.reshape(tokens, D)
    sa2, sb2 = sa.reshape(2, tokens, DA), sb.reshape(2, tokens, DB)
    dec = pl.pallas_call(
        dec_kernel,
        grid=(Fw // 256,),
        out_shape=jax.ShapeDtypeStruct((2, Fw, D), BF16),
        in_specs=[smem, pl.BlockSpec((tokens, 256), lambda i: (0, i)),
                  pl.BlockSpec((2, tokens, DA), lambda i: (0, 0, 0)), pl.BlockSpec((2, tokens, DB), lambda i: (0, 0, 0))],
        out_specs=pl.BlockSpec((2, 256, D), lambda i: (0, i, 0)),
        cost_estimate=pl.CostEstimate(flops=4 * tokens * Fw * D, bytes_accessed=12 * 2**20, transcendentals=0),
    )(live, acts2, sa2, sb2)
    enc = pl.pallas_call(
        enc_kernel,
        grid=(D // 384,),
        out_shape=jax.ShapeDtypeStruct((D, Fw), BF16),
        in_specs=[pl.BlockSpec((tokens, 384), lambda i: (0, i)), pl.BlockSpec((tokens, Fw), lambda i: (0, 0))],
        out_specs=pl.BlockSpec((384, Fw), lambda i: (i, 0)),
        cost_estimate=pl.CostEstimate(flops=2 * tokens * Fw * D, bytes_accessed=7 * 2**20, transcendentals=0),
    )(g2, low2)
    return enc[None], dec[None], bias


def solution(mesh):
    return jax.shard_map(
        step,
        mesh=mesh,
        in_specs=(
            P("layer", "tok", None),
            P("layer", None, ("feat", "tok")),
            P("layer", ("feat", "tok")),
            P("layer", None, ("feat", "tok")),
            P("layer", None, ("feat", "tok"), None),
            P(None, "tok", None),
            P(),
        ),
        out_specs=(
            P("layer", None, ("feat", "tok")),
            P("layer", None, ("feat", "tok"), None),
            P("layer", ("feat", "tok")),
        ),
        check_vma=False,
    )
```

time: 274 us -> 108 us (0.39)
  waiting for transfers between devices: 201 us -> 0 us
  Pallas kernels: 0 us -> 105 us
  matrix products: 36 us -> 0 us
  other arithmetic: 16.8 us -> 1.17 us
  between operations: 14.2 us -> 0.64 us
  local copies, waits for them, and re-layouts: 5.04 us -> 0.6 us
    psum x1 -> x0, waiting for transfers between devices: 164 us -> none  [shards(): lax.psum(partials * live_mask[:, None, None], ('layer', 'feat', 'tok'))]
    pallas_call x0 -> x3, Pallas kernels: none -> 105 us  [the longest x1 89.3 us: step(): pl.pallas_call(functools.partial(comm_kernel, cfg), out_shape=(jax.ShapeD...]
    all_gather x1 -> x0, waiting for transfers between devices: 37 us -> none  [shards(): gathered = lax.all_gather(sublevel_entries, 'tok', axis=1, tiled=True)[0]]
    dot_general x8 -> x0, matrix products: 36 us -> none  [the longest x2 10.3 us: shards(): jnp.einsum('td,fd->tf', scaled[desired_reconstruction], writeout_matrix[0...]
    broadcast_in_dim x1 -> x0, other arithmetic: 5.03 us -> none  [shards(): return (enc_grad[None], jnp.stack(dec_rows)[None], bias_grad[None])]
    mul x1 -> x0, other arithmetic: 4.32 us -> none  [shards(): partials * live_mask[:, None, None]]
    convert_element_type x2 -> x1, other arithmetic: 5.1 us -> 1.17 us  [step(): live = (lax.axis_index('layer') <= depths).astype(F32)]
    unnamed x19 -> x3, local copies, waits for them, and re-layouts: 4.47 us -> 0.6 us
  transfers between devices with their start and end apart: 2 -> 0, of which waited for: 2 -> 0; matrix products, arithmetic and copies ran while one was open for 0% -> 0% of each run, Pallas kernels for 0% -> 0%
where the time goes in v1:
time: 108 us
  Pallas kernels  105 us (97%)
  other arithmetic  1.17 us (1%)
    pallas_call x1, Pallas kernels, step(): pl.pallas_call(functools.partial(comm_kernel, cfg), out_shape=(jax.ShapeD...  89.3 us
    pallas_call x1, Pallas kernels, step(): pl.pallas_call(dec_kernel, grid=(Fw // 256,), out_shape=jax.ShapeDtypeStr...  9.9 us
    pallas_call x1, Pallas kernels, step(): pl.pallas_call(enc_kernel, grid=(D // 384,), out_shape=jax.ShapeDtypeStru...  6.19 us

profile of v1, /device:TPU:1, one launch (start us, length us, event | category | flops | bytes accessed | tf_op | source)
XLA Modules:
  0.0 107.8 jit_solution(16634614255652889179)
XLA Ops:
  0.6 1.2 %compare_convert_fusion.live_ref = f32[2]{0:T(128)} fusion(s32[2]{0:T(128)} %param.13, s32[]{:T(128)S(6)} %axis_index.15), kind=kLoop, calls=%fused_computation | loop fusion | flops 4 | bytes 20 | tf_op jit(solution)/shard_map/convert_element_type | solution.py:273
  1.8 89.3 %shard_map.94 = (f32[1,1024]{1,0:T(1,128)}, bf16[4,256,1152]{2,1,0:T(8,128)(2,1)}, bf16[4,256,1024]{2,1,0:T(8,128)(2,1)}, bf16[4,256,1024]{2,1,0:T(8,128)(2,1)},...) custom-call(f32[2]{0:T(128)} %compare_convert_fusion.live_ref, bf16[256,1152]{1,0:T(8,128)(2,1)} %bitcast.14, ...), custom_call_target="tpu_custom_call" | custom-call | tf_op jit(solution)/shard_map/pallas_call | solution.py:280
  91.1 6.2 %shard_map.95 = bf16[1152,1024]{1,0:T(8,128)(2,1)} custom-call(bf16[1024,1152]{1,0:T(8,128)(2,1)} %bitcast.16, bf16[1024,1024]{1,0:T(8,128)(2,1)} %bitcast.19), custom_call_target="tpu_custom_call" | custom-call | flops 2415919104 | bytes 7340032 | tf_op jit(solution)/shard_map/pallas_call | solution.py:318
  97.3 0.0 copy-start
  97.3 9.9 %shard_map.96 = bf16[2,1024,1152]{2,1,0:T(8,128)(2,1)} custom-call(f32[2]{0:T(128)} %compare_convert_fusion.live_ref, bf16[1024,1024]{1,0:T(8,128)(2,1)} %bitcast.17, bf16[2,1024,640]{2,1,0:T(8,128)(2,1)} %bitcast.15, bf16[2,1024,512]{2,1,0:T(8,128)(2,1)} %bitcast.18), custom_call_target="tpu_custom_call" | custom-call | flops 4831838208 | bytes 12582912 | tf_op jit(solution)/shard_map/pallas_call | solution.py:309
  107.2 0.0 copy-done
  107.2 0.6 copy.11
Async XLA Ops:
  97.3 9.9 %copy-start = (f32[1,1024]{1,0:T(1,128)S(1)}, f32[1,1024]{1,0:T(1,128)}, u32[]{:S(2)}) copy-start(f32[1,1024]{1,0:T(1,128)} %get-tuple-element.20) | copy-start | bytes 12292

commit v2 on v1

v2 whole, which is shorter than its diff:
```python
import functools
import math

import jax
import jax.numpy as jnp
from jax import lax
from jax.experimental import pallas as pl
from jax.experimental.pallas import tpu as pltpu
from jax.sharding import PartitionSpec as P

MESH = pl.DeviceIdType.MESH
F32, BF16 = jnp.float32, jnp.bfloat16
ROUNDS = 4
NT = (((1,), (1,)), ((), ()))
TN = (((0,), (0,)), ((), ()))
ORDER = (
    "F0", "F1", "E0", "F2", "10", "E1", "F3", "11", "E2", "20", "E3", "12", "21", "13", "30", "40", "22", "31",
    "23", "50", "32", "41", "33", "42", "60", "51", "70", "43", "52", "61", "53", "71", "62", "72", "63", "73",
)


def sent(R):
    slots = {}
    for name, count in (("g", 4), ("p", 1), ("a1", 3), ("b1", 3), ("a2", 3), ("b2", 3), ("x", 3),
                        ("ga1", 3), ("gb1", 3), ("ga2", 3), ("gb2", 3), ("fa", 1), ("fb", 1)):
        for i in range(count):
            slots[name, i] = len(slots)
    return slots


def comm_kernel(cfg, depth_ref, x_hbm, wr_hbm, off_ref, gate_hbm, wo_hbm, hid_hbm,
                bias_ref, g, acts, low, sa, sb,
                wr, gate, wo, hid, pk, cs, cr, s1a, s1b, r1a, r1b, k2a, k2b, s2a, s2b, r2a, r2b,
                k3, s3, r3, send_sem, recv_sem, in_sem, own_sem):
    R, TB, D, DA, Fw, inverse = cfg
    DB = D - DA
    M, PR, HB = 4 * TB, TB // 4, TB // 2
    slots = sent(R)
    layer, feat, x = lax.axis_index("layer"), lax.axis_index("feat"), lax.axis_index("tok")
    c = lax.rem(layer, 2)
    z = lax.rem(lax.div(layer, 2), 4)
    y = lax.div(layer, 8) * 2 + feat
    other = 1 - c

    def live_of(t):
        return (layer <= depth_ref[t]).astype(F32)

    def xpeer(o):
        return (layer, feat, lax.rem(x + o, 4))

    def zpeer(o):
        return (lax.div(layer, 8) * 8 + lax.rem(z + o, 4) * 2 + c, feat, x)

    def ypeer(o):
        yy = lax.rem(y + o, 4)
        return (lax.div(yy, 2) * 8 + z * 2 + c, lax.rem(yy, 2), x)

    def axes(j):
        pairs = ((zpeer, z), (ypeer, y))
        return pairs if j % 2 == 0 else pairs[::-1]

    partner = (lax.div(layer, 2) * 2 + other, feat, x)

    def at(index, size):
        return pl.ds(pl.multiple_of(index * size, size), size)

    def remote(j, name, i, src, dst, device):
        k = slots[name, i]
        return pltpu.make_async_remote_copy(
            src_ref=src, dst_ref=dst, send_sem=send_sem.at[j, k], recv_sem=recv_sem.at[j, k],
            device_id=device, device_id_type=MESH)

    started = []

    def send(j, name, i, src, dst, device):
        copy = remote(j, name, i, src, dst, device)
        copy.start()
        started.append(copy)

    def arrive(j, name, i, dst):
        remote(j, name, i, dst, dst, partner).wait_recv()

    loads = [pltpu.make_async_copy(a, b, in_sem.at[i]) for i, (a, b) in enumerate(
        ((wr_hbm, wr), (gate_hbm, gate), (wo_hbm, wo), (hid_hbm, hid)))]
    own = [pltpu.make_async_copy(x_hbm.at[pl.ds(j * TB, TB)], g.at[j, at(x, TB)], own_sem.at[j]) for j in range(R)]
    for j in range(R):
        own[j].start()
    for copy in loads:
        copy.start()
    bias_ref[...] = jnp.zeros_like(bias_ref)

    barrier = pltpu.get_barrier_semaphore()
    peers = [p(o) for p in (xpeer, ypeer, zpeer) for o in (1, 3, 2)] + [partner]
    for p in peers:
        pl.semaphore_signal(barrier, inc=1, device_id=p, device_id_type=MESH)
    pl.semaphore_wait(barrier, len(peers))

    def gather_own(j):
        src = x_hbm.at[pl.ds(j * TB, TB)]
        send(j, "g", 0, src, g.at[j, at(x, TB)], xpeer(1))
        send(j, "g", 1, src, g.at[j, at(x, TB)], xpeer(3))

    def stage_f(j):
        left, right = lax.rem(x + 3, 4), lax.rem(x + 1, 4)
        arrive(j, "g", 0, g.at[j, at(left, TB)])
        rows = pl.ds(pl.multiple_of(left * TB, TB), HB)
        send(j, "g", 2, g.at[j, rows], g.at[j, rows], xpeer(1))
        arrive(j, "g", 1, g.at[j, at(right, TB)])
        rows = pl.ds(pl.multiple_of(right * TB + HB, HB), HB)
        send(j, "g", 3, g.at[j, rows], g.at[j, rows], xpeer(3))
        if j + 2 < R:
            gather_own(j + 2)

    def stage_e(j):
        far = lax.rem(x + 2, 4)
        arrive(j, "g", 2, g.at[j, pl.ds(pl.multiple_of(far * TB, TB), HB)])
        arrive(j, "g", 3, g.at[j, pl.ds(pl.multiple_of(far * TB + HB, HB), HB)])
        own[j].wait()
        if j == 0:
            loads[0].wait()
            loads[1].wait()

        pre = jnp.dot(g[j], wr[...], preferred_element_type=F32) + off_ref[...]
        for t in range(4):
            rows = slice(t * TB, (t + 1) * TB)
            acts[j, rows] = (pre[rows] * gate[t, j * TB:(j + 1) * TB].astype(F32)).astype(BF16)
        if j == 0:
            loads[2].wait()
        part = jnp.dot(acts[j], wo[other], preferred_element_type=F32)
        cs[j] = (part * live_of(other)).astype(BF16)
        send(j, "p", 0, cs.at[j], cr.at[j], partner)
        pk[j] = jnp.dot(acts[j], wo[c], preferred_element_type=F32) * live_of(c)

    def stage_1(j):
        arrive(j, "p", 0, cr.at[j])
        (pa, qa), (pb, qb) = axes(j)
        s1a[j] = (pk[j, :, :DA] + cr[j, :, :DA].astype(F32)).astype(BF16)
        for o in (2, 1, 3):
            send(j, "a1", o - 1, s1a.at[j, at(lax.rem(qa + o, 4), TB)], r1a.at[j, o - 1], pa(o))
        s1b[j] = (pk[j, :, DA:] + cr[j, :, DA:].astype(F32)).astype(BF16)
        for o in (2, 1, 3):
            send(j, "b1", o - 1, s1b.at[j, at(lax.rem(qb + o, 4), TB)], r1b.at[j, o - 1], pb(o))

    def stage_2(j):
        (pa, qa), (pb, qb) = axes(j)
        for name, r1, q, k2, s2, r2, lanes, p, me, out in (
                ("a1", r1a, qa, k2a, s2a, r2a, slice(0, DA), pb, qb, "a2"),
                ("b1", r1b, qb, k2b, s2b, r2b, slice(DA, D), pa, qa, "b2")):
            total = pk[j, at(q, TB), lanes] + cr[j, at(q, TB), lanes].astype(F32)
            for i in (0, 2, 1):
                arrive(j, name, i, r1.at[j, i])
                total = total + r1[j, i].astype(F32)
            k2[j] = total
            s2[j] = total.astype(BF16)
            for o in (2, 1, 3):
                send(j, out, o - 1, s2.at[j, at(lax.rem(me + o, 4), PR)], r2.at[j, o - 1], p(o))

    def stage_3(j):
        if j == 0:
            loads[3].wait()
        (pa, qa), (pb, qb) = axes(j)
        for name, r2, me, k2, lanes, q in (("a2", r2a, qb, k2a, slice(0, DA), qa),
                                           ("b2", r2b, qa, k2b, slice(DA, D), qb)):
            total = k2[j, at(me, PR)]
            for i in (0, 2, 1):
                arrive(j, name, i, r2.at[j, i])
                total = total + r2[j, i].astype(F32)
            owner = (q == x).astype(F32)
            total = total - owner * hid[c, pl.ds(pl.multiple_of(j * TB + me * PR, PR), PR), lanes].astype(F32)
            k3[j, :, lanes] = total
            s3[j, :, lanes] = total.astype(BF16)
        for o in (2, 1, 3):
            send(j, "x", o - 1, s3.at[j], r3.at[j, o - 1], xpeer(o))

    def stage_4(j):
        total = k3[j]
        for i in (0, 2, 1):
            arrive(j, "x", i, r3.at[j, i])
            total = total + r3[j, i].astype(F32)
        scaled = (total * inverse).astype(BF16)
        (pa, qa), (pb, qb) = axes(j)
        arows = pl.ds(pl.multiple_of(qa * TB + qb * PR, PR), PR)
        brows = pl.ds(pl.multiple_of(qb * TB + qa * PR, PR), PR)
        sa[c, j, arows] = scaled[:, :DA]
        sb[c, j, brows] = scaled[:, DA:]
        for o in (2, 1, 3):
            send(j, "ga1", o - 1, sa.at[c, j, arows], sa.at[c, j, arows], pb(o))
            send(j, "gb1", o - 1, sb.at[c, j, brows], sb.at[c, j, brows], pa(o))

    def stage_5(j):
        (pa, qa), (pb, qb) = axes(j)
        for i, o in ((0, 3), (2, 1), (1, 2)):
            ra, rb = lax.rem(qa + o, 4), lax.rem(qb + o, 4)
            arrive(j, "ga1", i, sa.at[c, j, pl.ds(pl.multiple_of(qa * TB + rb * PR, PR), PR)])
            arrive(j, "gb1", i, sb.at[c, j, pl.ds(pl.multiple_of(qb * TB + ra * PR, PR), PR)])
        for o in (2, 1, 3):
            send(j, "ga2", o - 1, sa.at[c, j, at(qa, TB)], sa.at[c, j, at(qa, TB)], pa(o))
            send(j, "gb2", o - 1, sb.at[c, j, at(qb, TB)], sb.at[c, j, at(qb, TB)], pb(o))

    def stage_6(j):
        (pa, qa), (pb, qb) = axes(j)
        for i, o in ((0, 3), (2, 1), (1, 2)):
            arrive(j, "ga2", i, sa.at[c, j, at(lax.rem(qa + o, 4), TB)])
            arrive(j, "gb2", i, sb.at[c, j, at(lax.rem(qb + o, 4), TB)])
        send(j, "fa", 0, sa.at[c, j], sa.at[c, j], partner)
        send(j, "fb", 0, sb.at[c, j], sb.at[c, j], partner)

    def stage_7(j):
        arrive(j, "fa", 0, sa.at[other, j])
        arrive(j, "fb", 0, sb.at[other, j])

        total = jnp.zeros((M, Fw), F32)
        for t in range(2):
            part = lax.dot_general(sa[t, j], wo[t, :, :DA], NT, preferred_element_type=F32)
            part = part + lax.dot_general(sb[t, j], wo[t, :, DA:], NT, preferred_element_type=F32)
            total = total + live_of(t) * part
        for t in range(4):
            rows = slice(t * TB, (t + 1) * TB)
            pre = total[rows] * gate[t, j * TB:(j + 1) * TB].astype(F32)
            bias_ref[...] += jnp.sum(pre, axis=0, keepdims=True)
            low[j, rows] = pre.astype(BF16)

    gather_own(0)
    if R > 1:
        gather_own(1)
    stages = {"F": stage_f, "E": stage_e, "1": stage_1, "2": stage_2, "3": stage_3, "4": stage_4, "5": stage_5,
              "6": stage_6, "7": stage_7}
    for item in ORDER:
        stages[item[0]](int(item[1:]))
    for copy in started:
        copy.wait_send()


def grad_kernel(depth_ref, bias_ref, acts, x, low, sa, sb, enc_hbm, dec_hbm, bias_out, enc, dec, out_sem):
    layer = lax.axis_index("layer")
    Fw, D, DA = acts.shape[1], x.shape[1], sa.shape[-1]
    bias_out[...] = bias_ref[...]
    outs = []

    def put(src, dst):
        copy = pltpu.make_async_copy(src, dst, out_sem.at[len(outs)])
        copy.start()
        outs.append(copy)

    for t in range(2):
        live = (layer <= depth_ref[t]).astype(F32)
        for i in range(0, Fw, 512):
            rows = pl.ds(i, 512)
            got = lax.dot_general(acts[:, rows], sa[t], TN, preferred_element_type=F32)
            dec[t, rows, :DA] = (got * live).astype(BF16)
            got = lax.dot_general(acts[:, rows], sb[t], TN, preferred_element_type=F32)
            dec[t, rows, DA:] = (got * live).astype(BF16)
            put(dec.at[t, rows], dec_hbm.at[t, rows])
    for lo, hi in ((0, 512), (512, 896), (896, D)):
        rows = pl.ds(lo, hi - lo)
        got = lax.dot_general(x[:, rows], low[...], TN, preferred_element_type=F32)
        enc[rows] = got.astype(BF16)
        put(enc.at[rows], enc_hbm.at[rows])
    for copy in outs:
        copy.wait()


def step(entries, readin, offset, cutoff, writeout, hidden, depths):
    R = ROUNDS
    tokens, D = entries.shape[1] * 4, entries.shape[2]
    Fw = readin.shape[2]
    TB = tokens // 4 // R
    M, PR, DA = 4 * TB, TB // 4, 640
    DB = D - DA
    cfg = (R, TB, D, DA, Fw, 1.0 / math.sqrt(tokens))
    n_slots = len(sent(R))
    pin = functools.partial(pltpu.with_memory_space_constraint, memory_space=pltpu.HBM)
    hbm = pl.BlockSpec(memory_space=pltpu.HBM)
    vmem = pl.BlockSpec(memory_space=pltpu.VMEM)
    smem = pl.BlockSpec(memory_space=pltpu.SMEM)
    V = pltpu.VMEM
    bias, g, acts, low, sa, sb = pl.pallas_call(
        functools.partial(comm_kernel, cfg),
        out_shape=(
            jax.ShapeDtypeStruct((1, Fw), F32),
            jax.ShapeDtypeStruct((R, M, D), BF16),
            jax.ShapeDtypeStruct((R, M, Fw), BF16),
            jax.ShapeDtypeStruct((R, M, Fw), BF16),
            jax.ShapeDtypeStruct((2, R, M, DA), BF16),
            jax.ShapeDtypeStruct((2, R, M, DB), BF16),
        ),
        in_specs=[smem, hbm, hbm, vmem, hbm, hbm, hbm],
        out_specs=(vmem,) * 6,
        scratch_shapes=[
            V((D, Fw), BF16), V((4, tokens // 4, Fw), jnp.int32), V((2, Fw, D), BF16), V((2, tokens // 4, D), BF16),
            V((R, M, D), F32), V((R, M, D), BF16), V((R, M, D), BF16),
            V((R, M, DA), BF16), V((R, M, DB), BF16), V((R, 3, TB, DA), BF16), V((R, 3, TB, DB), BF16),
            V((R, TB, DA), F32), V((R, TB, DB), F32), V((R, TB, DA), BF16), V((R, TB, DB), BF16),
            V((R, 3, PR, DA), BF16), V((R, 3, PR, DB), BF16),
            V((R, PR, D), F32), V((R, PR, D), BF16), V((R, 3, PR, D), BF16),
            pltpu.SemaphoreType.DMA((R, n_slots)), pltpu.SemaphoreType.DMA((R, n_slots)),
            pltpu.SemaphoreType.DMA((4,)), pltpu.SemaphoreType.DMA((R,)),
        ],
        compiler_params=pltpu.CompilerParams(collective_id=0, has_side_effects=True, vmem_limit_bytes=36 * 2**20),
    )(pin(depths), pin(entries[0]), pin(readin[0]), pin(offset), pin(cutoff.reshape(4, tokens // 4, Fw)), pin(writeout[0]), pin(hidden))

    acts2, low2, g2 = acts.reshape(tokens, Fw), low.reshape(tokens, Fw), g.reshape(tokens, D)
    sa2, sb2 = sa.reshape(2, tokens, DA), sb.reshape(2, tokens, DB)
    enc, dec, bias = pl.pallas_call(
        grad_kernel,
        out_shape=(
            jax.ShapeDtypeStruct((D, Fw), BF16),
            jax.ShapeDtypeStruct((2, Fw, D), BF16),
            jax.ShapeDtypeStruct((1, Fw), F32),
        ),
        in_specs=[smem, vmem, vmem, vmem, vmem, vmem, vmem],
        out_specs=(hbm, hbm, vmem),
        scratch_shapes=[V((D, Fw), BF16), V((2, Fw, D), BF16), pltpu.SemaphoreType.DMA((7,))],
        compiler_params=pltpu.CompilerParams(vmem_limit_bytes=30 * 2**20),
        cost_estimate=pl.CostEstimate(flops=6 * tokens * Fw * D, bytes_accessed=18 * 2**20, transcendentals=0),
    )(pin(depths), bias, acts2, g2, low2, sa2, sb2)
    return enc[None], dec[None], bias


def solution(mesh):
    return jax.shard_map(
        step,
        mesh=mesh,
        in_specs=(
            P("layer", "tok", None),
            P("layer", None, ("feat", "tok")),
            P("layer", ("feat", "tok")),
            P("layer", None, ("feat", "tok")),
            P("layer", None, ("feat", "tok"), None),
            P(None, "tok", None),
            P(),
        ),
        out_specs=(
            P("layer", None, ("feat", "tok")),
            P("layer", None, ("feat", "tok"), None),
            P("layer", ("feat", "tok")),
        ),
        check_vma=False,
    )
```

time: 108 us -> 83.3 us (0.77)
  Pallas kernels: 105 us -> 82.3 us
  other arithmetic: 1.17 us -> 0 us
    pallas_call x1, Pallas kernels: 89.3 us -> 72 us  [step(): pl.pallas_call(functools.partial(comm_kernel, cfg), out_shape=(jax.ShapeD...]
    pallas_call x2 -> x1, Pallas kernels: 16.1 us -> 10.3 us  [step(): pl.pallas_call(grad_kernel, out_shape=(jax.ShapeDtypeStruct((D, Fw), BF16...]
    convert_element_type x1 -> x0, other arithmetic: 1.17 us -> none  [step(): live = (lax.axis_index('layer') <= depths).astype(F32)]
where the time goes in v2:
time: 83.3 us; the launch traced here: 83.1 us
  Pallas kernels  82.3 us (99%)
    pallas_call x1, Pallas kernels, step(): pl.pallas_call(functools.partial(comm_kernel, cfg), out_shape=(jax.ShapeD...  72 us
    pallas_call x1, Pallas kernels, step(): pl.pallas_call(grad_kernel, out_shape=(jax.ShapeDtypeStruct((D, Fw), BF16...  10.3 us

profile of v2, /device:TPU:1, one launch (start us, length us, event | category | flops | bytes accessed | tf_op | source)
XLA Modules:
  0.0 83.1 jit_solution(6726623933843917213)
XLA Ops:
  0.6 72.0 %shard_map.94 = (f32[1,1024]{1,0:T(1,128)S(1)}, bf16[4,256,1152]{2,1,0:T(8,128)(2,1)S(1)}, bf16[4,256,1024]{2,1,0:T(8,128)(2,1)S(1)}, bf16[4,256,1024]{2,1,0:T(8...) custom-call(s32[2]{0:T(128)} %depth_ref.3, bf16[256,1152]{1,0:T(8,128)(2,1)} %bitcast.19, ...), custom_call_target="tpu_custom_call" | custom-call | tf_op jit(solution)/shard_map/pallas_call | solution.py:277
  72.6 10.3 %shard_map.95 = (bf16[1152,1024]{1,0:T(8,128)(2,1)}, bf16[2,1024,1152]{2,1,0:T(8,128)(2,1)}, f32[1,1024]{1,0:T(1,128)}) custom-call(s32[2]{0:T(128)} %depth_ref.3, f32[1,1024]{1,0:T(1,128)S(1)} %get-tuple-element.12.bias_ref, bf16[1024,1024]{1,0:T(8,128)(2,1)S(1)} %bitcast.13, bf16[1024,1152]{1,0:T(8,128)(2,1)S(1)} %bitcast.12, ...), custom_call_target="tpu_custom_call" | custom-call | flops 7247757312 | bytes 18874368 | tf_op jit(solution)/shard_map/pallas_call | solution.py:304

commit v3 on v2

--- a/solution.py
+++ b/solution.py
@@ -11,11 +11,13 @@
 MESH = pl.DeviceIdType.MESH
 F32, BF16 = jnp.float32, jnp.bfloat16
 ROUNDS = 4
+EARLY = 2
 NT = (((1,), (1,)), ((), ()))
 TN = (((0,), (0,)), ((), ()))
 ORDER = (
     "F0", "F1", "E0", "F2", "10", "E1", "F3", "11", "E2", "20", "E3", "12", "21", "13", "30", "40", "22", "31",
-    "23", "50", "32", "41", "33", "42", "60", "51", "70", "43", "52", "61", "53", "71", "62", "72", "63", "73",
+    "23", "50", "32", "41", "33", "42", "60", "51", "43", "70", "52", "a0", "b0", "c0", "61", "53", "71", "62",
+    "a1", "b1", "72", "63", "c1", "73",
 )
 
 
@@ -29,8 +31,8 @@
 
 
 def comm_kernel(cfg, depth_ref, x_hbm, wr_hbm, off_ref, gate_hbm, wo_hbm, hid_hbm,
-                bias_ref, g, acts, low, sa, sb,
-                wr, gate, wo, hid, pk, cs, cr, s1a, s1b, r1a, r1b, k2a, k2b, s2a, s2b, r2a, r2b,
+                bias_ref, g, acts, low, sa, sb, accd, acce,
+                wr, gate, wo, hid, cs, cr, s1a, s1b, r1a, r1b, k2a, k2b, s2a, s2b, r2a, r2b,
                 k3, s3, r3, send_sem, recv_sem, in_sem, own_sem):
     R, TB, D, DA, Fw, inverse = cfg
     DB = D - DA
@@ -64,6 +66,9 @@
     def at(index, size):
         return pl.ds(pl.multiple_of(index * size, size), size)
 
+    def mine(j):
+        return pl.ds(j * M, M)
+
     def remote(j, name, i, src, dst, device):
         k = slots[name, i]
         return pltpu.make_async_remote_copy(
@@ -129,15 +134,15 @@
         part = jnp.dot(acts[j], wo[other], preferred_element_type=F32)
         cs[j] = (part * live_of(other)).astype(BF16)
         send(j, "p", 0, cs.at[j], cr.at[j], partner)
-        pk[j] = jnp.dot(acts[j], wo[c], preferred_element_type=F32) * live_of(c)
+        accd[1, mine(j)] = jnp.dot(acts[j], wo[c], preferred_element_type=F32) * live_of(c)
 
     def stage_1(j):
         arrive(j, "p", 0, cr.at[j])
         (pa, qa), (pb, qb) = axes(j)
-        s1a[j] = (pk[j, :, :DA] + cr[j, :, :DA].astype(F32)).astype(BF16)
+        s1a[j] = (accd[1, mine(j), :DA] + cr[j, :, :DA].astype(F32)).astype(BF16)
         for o in (2, 1, 3):
             send(j, "a1", o - 1, s1a.at[j, at(lax.rem(qa + o, 4), TB)], r1a.at[j, o - 1], pa(o))
-        s1b[j] = (pk[j, :, DA:] + cr[j, :, DA:].astype(F32)).astype(BF16)
+        s1b[j] = (accd[1, mine(j), DA:] + cr[j, :, DA:].astype(F32)).astype(BF16)
         for o in (2, 1, 3):
             send(j, "b1", o - 1, s1b.at[j, at(lax.rem(qb + o, 4), TB)], r1b.at[j, o - 1], pb(o))
 
@@ -146,7 +151,7 @@
         for name, r1, q, k2, s2, r2, lanes, p, me, out in (
                 ("a1", r1a, qa, k2a, s2a, r2a, slice(0, DA), pb, qb, "a2"),
                 ("b1", r1b, qb, k2b, s2b, r2b, slice(DA, D), pa, qa, "b2")):
-            total = pk[j, at(q, TB), lanes] + cr[j, at(q, TB), lanes].astype(F32)
+            total = accd[1, pl.ds(pl.multiple_of(j * M + q * TB, TB), TB), lanes] + cr[j, at(q, TB), lanes].astype(F32)
             for i in (0, 2, 1):
                 arrive(j, name, i, r1.at[j, i])
                 total = total + r1[j, i].astype(F32)
@@ -220,18 +225,31 @@
             bias_ref[...] += jnp.sum(pre, axis=0, keepdims=True)
             low[j, rows] = pre.astype(BF16)
 
+    def grad(t, j):
+        for i in range(0, Fw, 512):
+            rows = pl.ds(i, 512)
+            for ref, lanes in ((sa, slice(0, DA)), (sb, slice(DA, D))):
+                got = lax.dot_general(acts[j, :, rows], ref[t, j], TN, preferred_element_type=F32)
+                accd[t, rows, lanes] = got if j == 0 else accd[t, rows, lanes] + got
+
+    def stage_c(j):
+        for lo, hi in ((0, 512), (512, 896), (896, D)):
+            rows = pl.ds(lo, hi - lo)
+            got = lax.dot_general(g[j, :, rows], low[j], TN, preferred_element_type=F32)
+            acce[rows] = got if j == 0 else acce[rows] + got
+
     gather_own(0)
     if R > 1:
         gather_own(1)
     stages = {"F": stage_f, "E": stage_e, "1": stage_1, "2": stage_2, "3": stage_3, "4": stage_4, "5": stage_5,
-              "6": stage_6, "7": stage_7}
+              "6": stage_6, "7": stage_7, "a": functools.partial(grad, 0), "b": functools.partial(grad, 1), "c": stage_c}
     for item in ORDER:
         stages[item[0]](int(item[1:]))
     for copy in started:
         copy.wait_send()
 
 
-def grad_kernel(depth_ref, bias_ref, acts, x, low, sa, sb, enc_hbm, dec_hbm, bias_out, enc, dec, out_sem):
+def grad_kernel(skip, depth_ref, bias_ref, acts, x, low, sa, sb, accd, acce, enc_hbm, dec_hbm, bias_out, enc, dec, out_sem):
     layer = lax.axis_index("layer")
     Fw, D, DA = acts.shape[1], x.shape[1], sa.shape[-1]
     bias_out[...] = bias_ref[...]
@@ -242,19 +260,19 @@
         copy.start()
         outs.append(copy)
 
+    late = slice(skip, acts.shape[0])
     for t in range(2):
         live = (layer <= depth_ref[t]).astype(F32)
         for i in range(0, Fw, 512):
             rows = pl.ds(i, 512)
-            got = lax.dot_general(acts[:, rows], sa[t], TN, preferred_element_type=F32)
-            dec[t, rows, :DA] = (got * live).astype(BF16)
-            got = lax.dot_general(acts[:, rows], sb[t], TN, preferred_element_type=F32)
-            dec[t, rows, DA:] = (got * live).astype(BF16)
+            for ref, lanes in ((sa, slice(0, DA)), (sb, slice(DA, D))):
+                got = lax.dot_general(acts[late, rows], ref[t, late], TN, preferred_element_type=F32)
+                dec[t, rows, lanes] = ((accd[t, rows, lanes] + got) * live).astype(BF16)
             put(dec.at[t, rows], dec_hbm.at[t, rows])
     for lo, hi in ((0, 512), (512, 896), (896, D)):
         rows = pl.ds(lo, hi - lo)
-        got = lax.dot_general(x[:, rows], low[...], TN, preferred_element_type=F32)
-        enc[rows] = got.astype(BF16)
+        got = lax.dot_general(x[late, rows], low[late], TN, preferred_element_type=F32)
+        enc[rows] = (acce[rows] + got).astype(BF16)
         put(enc.at[rows], enc_hbm.at[rows])
     for copy in outs:
         copy.wait()
@@ -274,7 +292,7 @@
     vmem = pl.BlockSpec(memory_space=pltpu.VMEM)
     smem = pl.BlockSpec(memory_space=pltpu.SMEM)
     V = pltpu.VMEM
-    bias, g, acts, low, sa, sb = pl.pallas_call(
+    bias, g, acts, low, sa, sb, accd, acce = pl.pallas_call(
         functools.partial(comm_kernel, cfg),
         out_shape=(
             jax.ShapeDtypeStruct((1, Fw), F32),
@@ -283,12 +301,14 @@
             jax.ShapeDtypeStruct((R, M, Fw), BF16),
             jax.ShapeDtypeStruct((2, R, M, DA), BF16),
             jax.ShapeDtypeStruct((2, R, M, DB), BF16),
+            jax.ShapeDtypeStruct((2, Fw, D), F32),
+            jax.ShapeDtypeStruct((D, Fw), F32),
         ),
         in_specs=[smem, hbm, hbm, vmem, hbm, hbm, hbm],
-        out_specs=(vmem,) * 6,
+        out_specs=(vmem,) * 8,
         scratch_shapes=[
             V((D, Fw), BF16), V((4, tokens // 4, Fw), jnp.int32), V((2, Fw, D), BF16), V((2, tokens // 4, D), BF16),
-            V((R, M, D), F32), V((R, M, D), BF16), V((R, M, D), BF16),
+            V((R, M, D), BF16), V((R, M, D), BF16),
             V((R, M, DA), BF16), V((R, M, DB), BF16), V((R, 3, TB, DA), BF16), V((R, 3, TB, DB), BF16),
             V((R, TB, DA), F32), V((R, TB, DB), F32), V((R, TB, DA), BF16), V((R, TB, DB), BF16),
             V((R, 3, PR, DA), BF16), V((R, 3, PR, DB), BF16),
@@ -296,24 +316,24 @@
             pltpu.SemaphoreType.DMA((R, n_slots)), pltpu.SemaphoreType.DMA((R, n_slots)),
             pltpu.SemaphoreType.DMA((4,)), pltpu.SemaphoreType.DMA((R,)),
         ],
-        compiler_params=pltpu.CompilerParams(collective_id=0, has_side_effects=True, vmem_limit_bytes=36 * 2**20),
+        compiler_params=pltpu.CompilerParams(collective_id=0, has_side_effects=True, vmem_limit_bytes=27 * 2**20),
     )(pin(depths), pin(entries[0]), pin(readin[0]), pin(offset), pin(cutoff.reshape(4, tokens // 4, Fw)), pin(writeout[0]), pin(hidden))
 
     acts2, low2, g2 = acts.reshape(tokens, Fw), low.reshape(tokens, Fw), g.reshape(tokens, D)
     sa2, sb2 = sa.reshape(2, tokens, DA), sb.reshape(2, tokens, DB)
     enc, dec, bias = pl.pallas_call(
-        grad_kernel,
+        functools.partial(grad_kernel, EARLY * M),
         out_shape=(
             jax.ShapeDtypeStruct((D, Fw), BF16),
             jax.ShapeDtypeStruct((2, Fw, D), BF16),
             jax.ShapeDtypeStruct((1, Fw), F32),
         ),
-        in_specs=[smem, vmem, vmem, vmem, vmem, vmem, vmem],
+        in_specs=[smem] + [vmem] * 8,
         out_specs=(hbm, hbm, vmem),
         scratch_shapes=[V((D, Fw), BF16), V((2, Fw, D), BF16), pltpu.SemaphoreType.DMA((7,))],
-        compiler_params=pltpu.CompilerParams(vmem_limit_bytes=30 * 2**20),
+        compiler_params=pltpu.CompilerParams(vmem_limit_bytes=14 * 2**20),
         cost_estimate=pl.CostEstimate(flops=6 * tokens * Fw * D, bytes_accessed=18 * 2**20, transcendentals=0),
-    )(pin(depths), bias, acts2, g2, low2, sa2, sb2)
+    )(pin(depths), bias, acts2, g2, low2, sa2, sb2, accd, acce)
     return enc[None], dec[None], bias
 
 

time: 83.3 us -> 78.2 us (0.939)
  Pallas kernels: 82.3 us -> 77.3 us
    pallas_call x1, Pallas kernels: 10.3 us -> 6.36 us  [step(): pl.pallas_call(functools.partial(grad_kernel, EARLY * M), out_shape=(jax....]
    pallas_call x1, Pallas kernels: 72 us -> 70.9 us  [step(): pl.pallas_call(functools.partial(comm_kernel, cfg), out_shape=(jax.ShapeD...]
where the time goes in v3:
time: 78.2 us; the launch traced here: 78.1 us
  Pallas kernels  77.3 us (99%)
  between operations  0.8 us (1%)
    pallas_call x1, Pallas kernels, step(): pl.pallas_call(functools.partial(comm_kernel, cfg), out_shape=(jax.ShapeD...  70.9 us
    pallas_call x1, Pallas kernels, step(): pl.pallas_call(functools.partial(grad_kernel, EARLY * M), out_shape=(jax....  6.36 us

profile of v3, /device:TPU:1, one launch (start us, length us, event | category | flops | bytes accessed | tf_op | source)
XLA Modules:
  0.0 78.1 jit_solution(17268445735781964810)
XLA Ops:
  0.6 70.9 %shard_map.94 = (f32[1,1024]{1,0:T(1,128)S(1)}, bf16[4,256,1152]{2,1,0:T(8,128)(2,1)S(1)}, bf16[4,256,1024]{2,1,0:T(8,128)(2,1)S(1)}, bf16[4,256,1024]{2,1,0:T(8...) custom-call(s32[2]{0:T(128)} %depth_ref.3, ...), custom_call_target="tpu_custom_call" | custom-call | tf_op jit(solution)/shard_map/pallas_call | solution.py:295
  71.6 6.4 %shard_map.95 = (bf16[1152,1024]{1,0:T(8,128)(2,1)}, bf16[2,1024,1152]{2,1,0:T(8,128)(2,1)}, f32[1,1024]{1,0:T(1,128)}) custom-call(s32[2]{0:T(128)} %depth_ref.3, f32[1,1024]{1,0:T(1,128)S(1)} %get-tuple-element.14.bias_ref, bf16[1024,1024]{1,0:T(8,128)(2,1)S(1)} %bitcast.13, bf16[1024,1152]{1,0:T(8,128)(2,1)S(1)} %bitcast.12, ...), custom_call_target="tpu_custom_call" | custom-call | flops 7247757312 | bytes 18874368 | tf_op jit(solution)/shard_map/pallas_call | solution.py:324

commit v4 on v3

--- a/solution.py
+++ b/solution.py
@@ -15,8 +15,8 @@
 NT = (((1,), (1,)), ((), ()))
 TN = (((0,), (0,)), ((), ()))
 ORDER = (
-    "F0", "F1", "E0", "F2", "10", "E1", "F3", "11", "E2", "20", "E3", "12", "21", "13", "30", "40", "22", "31",
-    "23", "50", "32", "41", "33", "42", "60", "51", "43", "70", "52", "a0", "b0", "c0", "61", "53", "71", "62",
+    "F0", "F1", "E0", "F2", "10", "E1", "F3", "11", "E2", "20", "12", "E3", "13", "21", "30", "22", "40", "23",
+    "31", "32", "50", "33", "41", "42", "43", "60", "51", "52", "70", "a0", "53", "b0", "c0", "61", "71", "62",
     "a1", "b1", "72", "63", "c1", "73",
 )
 
@@ -33,7 +33,7 @@
 def comm_kernel(cfg, depth_ref, x_hbm, wr_hbm, off_ref, gate_hbm, wo_hbm, hid_hbm,
                 bias_ref, g, acts, low, sa, sb, accd, acce,
                 wr, gate, wo, hid, cs, cr, s1a, s1b, r1a, r1b, k2a, k2b, s2a, s2b, r2a, r2b,
-                k3, s3, r3, send_sem, recv_sem, in_sem, own_sem):
+                k3, s3, r3, half, send_sem, recv_sem, in_sem, own_sem):
     R, TB, D, DA, Fw, inverse = cfg
     DB = D - DA
     M, PR, HB = 4 * TB, TB // 4, TB // 2
@@ -202,6 +202,11 @@
             send(j, "ga2", o - 1, sa.at[c, j, at(qa, TB)], sa.at[c, j, at(qa, TB)], pa(o))
             send(j, "gb2", o - 1, sb.at[c, j, at(qb, TB)], sb.at[c, j, at(qb, TB)], pb(o))
 
+    def act_grad(t, j):
+        part = lax.dot_general(sa[t, j], wo[t, :, :DA], NT, preferred_element_type=F32)
+        part = part + lax.dot_general(sb[t, j], wo[t, :, DA:], NT, preferred_element_type=F32)
+        return live_of(t) * part
+
     def stage_6(j):
         (pa, qa), (pb, qb) = axes(j)
         for i, o in ((0, 3), (2, 1), (1, 2)):
@@ -210,15 +215,17 @@
         send(j, "fa", 0, sa.at[c, j], sa.at[c, j], partner)
         send(j, "fb", 0, sb.at[c, j], sb.at[c, j], partner)
 
+        if j == R - 1:
+            half[...] = act_grad(c, j)
+
     def stage_7(j):
         arrive(j, "fa", 0, sa.at[other, j])
         arrive(j, "fb", 0, sb.at[other, j])
 
-        total = jnp.zeros((M, Fw), F32)
-        for t in range(2):
-            part = lax.dot_general(sa[t, j], wo[t, :, :DA], NT, preferred_element_type=F32)
-            part = part + lax.dot_general(sb[t, j], wo[t, :, DA:], NT, preferred_element_type=F32)
-            total = total + live_of(t) * part
+        if j == R - 1:
+            total = half[...] + act_grad(other, j)
+        else:
+            total = act_grad(0, j) + act_grad(1, j)
         for t in range(4):
             rows = slice(t * TB, (t + 1) * TB)
             pre = total[rows] * gate[t, j * TB:(j + 1) * TB].astype(F32)
@@ -312,7 +319,7 @@
             V((R, M, DA), BF16), V((R, M, DB), BF16), V((R, 3, TB, DA), BF16), V((R, 3, TB, DB), BF16),
             V((R, TB, DA), F32), V((R, TB, DB), F32), V((R, TB, DA), BF16), V((R, TB, DB), BF16),
             V((R, 3, PR, DA), BF16), V((R, 3, PR, DB), BF16),
-            V((R, PR, D), F32), V((R, PR, D), BF16), V((R, 3, PR, D), BF16),
+            V((R, PR, D), F32), V((R, PR, D), BF16), V((R, 3, PR, D), BF16), V((M, Fw), F32),
             pltpu.SemaphoreType.DMA((R, n_slots)), pltpu.SemaphoreType.DMA((R, n_slots)),
             pltpu.SemaphoreType.DMA((4,)), pltpu.SemaphoreType.DMA((R,)),
         ],

time: 78.2 us -> 76.8 us (0.982)
  Pallas kernels: 77.3 us -> 75.8 us
    pallas_call x1, Pallas kernels: 70.9 us -> 69.5 us  [step(): pl.pallas_call(functools.partial(comm_kernel, cfg), out_shape=(jax.ShapeD...]
where the time goes in v4:
time: 76.8 us; the launch traced here: 76.6 us
  Pallas kernels  75.8 us (99%)
  between operations  0.8 us (1%)
    pallas_call x1, Pallas kernels, step(): pl.pallas_call(functools.partial(comm_kernel, cfg), out_shape=(jax.ShapeD...  69.5 us
    pallas_call x1, Pallas kernels, step(): pl.pallas_call(functools.partial(grad_kernel, EARLY * M), out_shape=(jax....  6.36 us

profile of v4, /device:TPU:1, one launch (start us, length us, event | category | flops | bytes accessed | tf_op | source)
XLA Modules:
  0.0 76.6 jit_solution(7784689526216463355)
XLA Ops:
  0.6 69.5 %shard_map.94 = (f32[1,1024]{1,0:T(1,128)S(1)}, bf16[4,256,1152]{2,1,0:T(8,128)(2,1)S(1)}, bf16[4,256,1024]{2,1,0:T(8,128)(2,1)S(1)}, bf16[4,256,1024]{2,1,0:T(8...) custom-call(s32[2]{0:T(128)} %depth_ref.3, ...), custom_call_target="tpu_custom_call" | custom-call | tf_op jit(solution)/shard_map/pallas_call | solution.py:302
  70.1 6.4 %shard_map.95 = (bf16[1152,1024]{1,0:T(8,128)(2,1)}, bf16[2,1024,1152]{2,1,0:T(8,128)(2,1)}, f32[1,1024]{1,0:T(1,128)}) custom-call(s32[2]{0:T(128)} %depth_ref.3, f32[1,1024]{1,0:T(1,128)S(1)} %get-tuple-element.14.bias_ref, bf16[1024,1024]{1,0:T(8,128)(2,1)S(1)} %bitcast.13, bf16[1024,1152]{1,0:T(8,128)(2,1)S(1)} %bitcast.12, ...), custom_call_target="tpu_custom_call" | custom-call | flops 7247757312 | bytes 18874368 | tf_op jit(solution)/shard_map/pallas_call | solution.py:331
